TPU v7x, 32 devices: a whole 2x2x4 slice. The times are simulated.
32 devices in a mesh: groups: 2 (over y), ctx: 4 (over z), tp: 2 (over x), sub: 2 (over core).
Axes of the slice: x: 2, y: 2, z: 4, core: 2. Of those that a mesh axis runs over, the one named last changes fastest.
Arguments:
- queries: bfloat16 [3072, 8192], P(('groups', 'ctx'), ('tp', 'sub')), parts along dimension 0, may hold values from -200 to 200
- keys: bfloat16 [3072, 1024], P(('groups', 'ctx'), ('tp', 'sub')), parts along dimension 0, may hold values from -6 to 6
- values: bfloat16 [3072, 1024], P(('groups', 'ctx'), ('tp', 'sub')), parts along dimension 0, may hold values from -6 to 6
- segment_ids: int32 [3072], P(('groups', 'ctx')), parts along dimension 0, may hold values from 0 to 8, as said below
Outputs:
- attended: bfloat16 [3072, 8192], P(('groups', 'ctx'), ('tp', 'sub')), parts along dimension 0
There are 2 independent parts, one for each index of `groups`. A program takes and returns all parts, laid end to end along the dimension named above; each array names one. Nothing has to cross between parts.
Inputs may be any that keep to these rules, and one draw needn't show every extreme that they name: segment_ids is 0 on the first 384 tokens; after them exactly 8 chains 1, 2, ..., 8 follow in order and fill the row, each a run of 96 to 192 tokens, one of them exactly 192.
All inputs are finite; a program needn't handle non-finite values.
Results may differ from a plain program's by a relative error of at most 0.0041.
Values may be sent and summed in bfloat16 or wider, within the bound.
No kernel may reach another device: no remote copies, remote signals or barrier semaphores. Data moves between devices by JAX's collectives and lax.ppermute only.
A program may use at most 64 MiB of HBM per device.

v0:
```python
import jax
import jax.numpy as jnp
from jax import lax
from jax.sharding import PartitionSpec as P

HEAD_DIM = 128
GROUP = 8


def attend_block(
    running,
    key_block,
    value_block,
    segment_block,
    first_row,
    query_heads,
    query_places,
    query_segment,
):
    number = key_block.shape[0]
    heads_here = key_block.shape[1] // HEAD_DIM
    key_places = first_row + jnp.arange(number, dtype=jnp.int32)
    same = (segment_block[None, :] == query_segment[:, None]) | (segment_block[None, :] == 0)
    visible = (key_places[None, :] <= query_places[:, None]) & same
    key_heads = key_block.reshape(number, heads_here, HEAD_DIM)
    value_heads = value_block.reshape(number, heads_here, HEAD_DIM)

    def compute(state):
        row_peak, row_total, weighted = state
        scores = jnp.einsum(
            "qhgd,khd->hgqk", query_heads, key_heads, preferred_element_type=jnp.float32
        ) * HEAD_DIM ** (-0.5)
        scores = jnp.where(visible[None, None], scores, -1e30)
        new_peak = jnp.maximum(row_peak, jnp.max(scores, axis=-1))
        factor = jnp.exp(row_peak - new_peak)
        weights = jnp.where(visible[None, None], jnp.exp(scores - new_peak[..., None]), 0.0)
        new_total = row_total * factor + jnp.sum(weights, axis=-1)
        added = jnp.einsum(
            "hgqk,khd->hgqd",
            weights.astype(jnp.bfloat16),
            value_heads,
            preferred_element_type=jnp.float32,
        )
        return (new_peak, new_total, weighted * factor[..., None] + added)

    return lax.cond(jnp.any(visible), compute, lambda state: state, running)


def per_device(queries, keys, values, segment_ids):
    row_count = queries.shape[0]
    heads_here = keys.shape[1] // HEAD_DIM
    my_index = lax.axis_index("ctx")
    query_places = my_index * row_count + jnp.arange(row_count, dtype=jnp.int32)
    query_heads = queries.reshape(row_count, heads_here, GROUP, HEAD_DIM)
    initial = (
        jnp.full((heads_here, GROUP, row_count), -1e30, jnp.float32),
        jnp.zeros((heads_here, GROUP, row_count), jnp.float32),
        jnp.zeros((heads_here, GROUP, row_count, HEAD_DIM), jnp.float32),
    )
    key_all = lax.all_gather(keys, "ctx", axis=0, tiled=True)
    value_all = lax.all_gather(values, "ctx", axis=0, tiled=True)
    segment_all = lax.all_gather(segment_ids, "ctx", axis=0, tiled=True)
    blocks = max(1, key_all.shape[0] // row_count)
    width_rows = key_all.shape[0] // blocks

    def turn(number, state):
        offset = number * width_rows
        key_part = lax.dynamic_slice_in_dim(key_all, offset, width_rows, 0)
        value_part = lax.dynamic_slice_in_dim(value_all, offset, width_rows, 0)
        segment_part = lax.dynamic_slice_in_dim(segment_all, offset, width_rows, 0)
        return attend_block(
            state,
            key_part,
            value_part,
            segment_part,
            offset,
            query_heads,
            query_places,
            segment_ids,
        )

    final = lax.fori_loop(0, blocks, turn, initial)
    row_peak, row_total, weighted = final
    mixed = weighted / row_total[..., None]
    mixed = jnp.transpose(mixed, (2, 0, 1, 3)).reshape(row_count, heads_here * GROUP * HEAD_DIM)
    return mixed.astype(jnp.bfloat16)


def solution(mesh):
    placed = (
        P(("groups", "ctx"), ("tp", "sub")),
        P(("groups", "ctx"), ("tp", "sub")),
        P(("groups", "ctx"), ("tp", "sub")),
        P(("groups", "ctx")),
    )
    return jax.shard_map(
        per_device,
        mesh=mesh,
        in_specs=placed,
        out_specs=P(("groups", "ctx"), ("tp", "sub")),
        check_vma=False,
    )
```

profile of v0, /device:TPU:22, one launch (start us, length us, event | category | flops | bytes accessed | tf_op | source)
XLA Modules:
  0.0 98.1 jit_solution(1589817121826386383)
XLA Ops:
  0.0 0.7 reshape.39
  0.7 10.3 %all-gather = s32[4,1,384]{2,1,0:T(1,128)S(1)} all-gather(s32[1,1,384]{2,1,0:T(1,128)S(1)} %reshape.39), channel_id=1, replica_groups=mesh['groups'=2,'ctx'=4,'tp'=2,'sub'=2] {'ctx'}, dimensions={0}, use_global_device_ids=true | all-gather | bytes 7680 | tf_op jit(solution)/shard_map/all_gather | solution.py:62
  11.0 1.1 %copy.18 = bf16[384,256]{0,1:T(8,128)(2,1)S(1)} copy(bf16[384,256]{1,0:T(8,128)(2,1)} %param.9) | data formatting | bytes 393216 | tf_op args[1]
  12.1 1.1 %copy.20 = bf16[384,256]{0,1:T(8,128)(2,1)S(1)} copy(bf16[384,256]{1,0:T(8,128)(2,1)} %param.10) | data formatting | bytes 393216 | tf_op args[2]
  13.2 18.8 %all_gather.11 = bf16[1536,256]{0,1:T(8,128)(2,1)} all-gather(bf16[384,256]{0,1:T(8,128)(2,1)S(1)} %copy.20), channel_id=1, replica_groups=mesh['groups'=2,'ctx'=4,'tp'=2,'sub'=2] {'ctx'}, dimensions={0}, use_global_device_ids=true | all-gather | bytes 983040 | tf_op jit(solution)/shard_map/all_gather | solution.py:61
  32.0 17.9 %all_gather.10 = bf16[1536,256]{0,1:T(8,128)(2,1)} all-gather(bf16[384,256]{0,1:T(8,128)(2,1)S(1)} %copy.18), channel_id=1, replica_groups=mesh['groups'=2,'ctx'=4,'tp'=2,'sub'=2] {'ctx'}, dimensions={0}, use_global_device_ids=true | all-gather | bytes 983040 | tf_op jit(solution)/shard_map/all_gather | solution.py:60
  49.9 0.0 copy-start.2
  49.9 1.9 %copy.19 = bf16[384,2048]{0,1:T(8,128)(2,1)S(1)} copy(bf16[384,2048]{1,0:T(8,128)(2,1)} %param.8) | data formatting | bytes 3145728 | tf_op args[0]
  51.8 1.0 copy.21
  52.8 2.0 %broadcast_in_dim.53 = f32[2,8,384,128]{3,2,1,0:T(8,128)} broadcast(f32[]{:T(128)} %constant.68.clone.1), dimensions={} | broadcast | bytes 3145732 | tf_op jit(solution)/shard_map/broadcast_in_dim | solution.py:58
  54.8 0.0 copy-done.2
  54.8 38.4 %while.18 = (s32[]{:T(128)}, f32[2,8,384]{2,1,0:T(8,128)S(1)}, f32[2,8,384]{2,1,0:T(8,128)S(1)}, f32[2,8,384,128]{3,2,1,0:T(8,128)}, s32[1536]{0:T(1024)S(1)}, /...) while((s32[]{:T(128)}, f32[2,8,384]{2,1,0:T(8,128)S(1)}, ...), condition=%wide.region_6.7_spmd.clone, body=%wide.region_0.6_spmd.clone.sunk | while | flops 1240953984 | bytes 63517816 | solution.py:82
  54.8 0.1 broadcast_compare_fusion.2
  54.9 0.9 fusion.19
  56.4 10.6 %conditional.3 = ((f32[2,8,384]{2,1,0:T(8,128)S(1)}, f32[2,8,384]{2,1,0:T(8,128)S(1)}, f32[2,8,384,128]{3,2,1,0:T(8,128)})) conditional(s32[]{:T(128)} %convert_element_type.33, (f32[2,8,384]{2,1,0:T(8,128)S(1)}, f32[2,8,384]{2,1,0:T(8,128)S(1)}, f32[2,8,384,128]{3,2,1,0:T(8,128)}) %tuple.60, (pred[384,384]{0,1:T(8,128)(4,1)S(1)}, ...), branch_computations={%region_2.0_spmd, %region_3.5_spmd} | conditional | flops 1240215552 | bytes 63357020 | solution.py:46
  56.4 1.1 %constant_dynamic-slice_fusion = (bf16[384,256]{0,1:T(8,128)(2,1)S(1)}, bf16[384,256]{0,1:T(8,128)(2,1)S(1)}) fusion(bf16[1536,256]{0,1:T(8,128)(2,1)} %get-tuple-element.240, s32[]{:T(128)} %get-tuple-element.236, bf16[1536,256]{0,1:T(8,128)(2,1)} %get-tuple-element.235), kind=kLoop, calls=%fused_computation.11 | loop fusion | bytes 786436 | tf_op jit(solution)/shard_map/while/body/eval_jaxpr/dynamic_slice | solution.py:69
  57.5 1.7 %fusion.2 = (f32[2,8,384]{2,1,0:T(8,128)S(1)}, f32[2,384,384,8]{2,1,3,0:T(8,128)S(1)}) fusion(pred[384,384]{0,1:T(8,128)(4,1)S(1)} %get-tuple-element.234, bf16[384,2,128,1]{0,2,3,1:T(8,128)(2,1)S(1)} %bitcast.34, bf16[384,2,8,128]{3,0,2,1:T(8,128)(2,1)S(1)} %get-tuple-element.237), kind=kOutput, calls=%fused_computation.3 | convolution fusion | flops 611051520 | bytes 11378688 | tf_op jit(solution)/shard_map/while/body/eval_jaxpr/cond/branch_1_fun/qhgd,khd->hgqk/dot_general | solution.py:30
  59.2 0.0 copy-start
  59.2 2.3 %fusion.4 = f32[2,8,384]{2,1,0:T(8,128)S(1)} fusion(f32[2,384,384,8]{2,1,3,0:T(8,128)S(1)} %get-tuple-element.332, f32[2,8,384]{2,1,0:T(8,128)S(1)} %max.4, pred[384,384]{0,1:T(8,128)(4,1)S(1)} %get-tuple-element.234), kind=kLoop, calls=%fused_computation.5 | loop fusion | flops 11790336 | bytes 9633792 | tf_op jit(solution)/shard_map/while/body/eval_jaxpr/cond/branch_1_fun/reduce_sum | solution.py:37
  61.5 0.0 copy-done
  61.5 3.8 %multiply_add_fusion = f32[2,8,384,128]{3,2,1,0:T(8,128)S(1)} fusion(f32[2,8,384,128]{3,2,1,0:T(8,128)S(1)} %copy-done, bf16[384,2,128,1]{0,2,3,1:T(8,128)(2,1)S(1)} %bitcast.37, f32[2,384,384,8]{2,1,3,0:T(8,128)S(1)} %get-tuple-element.332, f32[2,8,384]{2,1,0:T(8,128)S(1)} %max.4, pred[384,384]{0,1:T(8,128)(4,1)S(1)} %get-tuple-element.234, ...), kind=kOutput, calls=%fused_computation.8 | convolution fusion | flops 617349120 | bytes 16121856 | tf_op jit(solution)/shard_map/while/body/eval_jaxpr/cond/branch_1_fun/hgqk,khd->hgqd/dot_general | solution.py:38
  65.4 0.0 copy-start.1
  65.4 1.6 %copy-done.1 = f32[2,8,384,128]{3,2,1,0:T(8,128)} copy-done((f32[2,8,384,128]{3,2,1,0:T(8,128)}, f32[2,8,384,128]{3,2,1,0:T(8,128)S(1)}, u32[]{:S(2)}) %copy-start.1) | copy-done | bytes 3145752 | tf_op jit(solution)/shard_map/while/body/eval_jaxpr/cond
  67.0 0.1 broadcast_compare_fusion.2
  67.1 0.9 fusion.19
  68.6 10.6 %conditional.3 = ((f32[2,8,384]{2,1,0:T(8,128)S(1)}, f32[2,8,384]{2,1,0:T(8,128)S(1)}, f32[2,8,384,128]{3,2,1,0:T(8,128)})) conditional(s32[]{:T(128)} %convert_element_type.33, (f32[2,8,384]{2,1,0:T(8,128)S(1)}, f32[2,8,384]{2,1,0:T(8,128)S(1)}, f32[2,8,384,128]{3,2,1,0:T(8,128)}) %tuple.60, (pred[384,384]{0,1:T(8,128)(4,1)S(1)}, ...), branch_computations={%region_2.0_spmd, %region_3.5_spmd} | conditional | flops 1240215552 | bytes 63357020 | solution.py:46
  68.6 1.1 %constant_dynamic-slice_fusion = (bf16[384,256]{0,1:T(8,128)(2,1)S(1)}, bf16[384,256]{0,1:T(8,128)(2,1)S(1)}) fusion(bf16[1536,256]{0,1:T(8,128)(2,1)} %get-tuple-element.240, s32[]{:T(128)} %get-tuple-element.236, bf16[1536,256]{0,1:T(8,128)(2,1)} %get-tuple-element.235), kind=kLoop, calls=%fused_computation.11 | loop fusion | bytes 786436 | tf_op jit(solution)/shard_map/while/body/eval_jaxpr/dynamic_slice | solution.py:69
  69.7 1.7 %fusion.2 = (f32[2,8,384]{2,1,0:T(8,128)S(1)}, f32[2,384,384,8]{2,1,3,0:T(8,128)S(1)}) fusion(pred[384,384]{0,1:T(8,128)(4,1)S(1)} %get-tuple-element.234, bf16[384,2,128,1]{0,2,3,1:T(8,128)(2,1)S(1)} %bitcast.34, bf16[384,2,8,128]{3,0,2,1:T(8,128)(2,1)S(1)} %get-tuple-element.237), kind=kOutput, calls=%fused_computation.3 | convolution fusion | flops 611051520 | bytes 11378688 | tf_op jit(solution)/shard_map/while/body/eval_jaxpr/cond/branch_1_fun/qhgd,khd->hgqk/dot_general | solution.py:30
  71.4 0.0 copy-start
  71.5 2.3 %fusion.4 = f32[2,8,384]{2,1,0:T(8,128)S(1)} fusion(f32[2,384,384,8]{2,1,3,0:T(8,128)S(1)} %get-tuple-element.332, f32[2,8,384]{2,1,0:T(8,128)S(1)} %max.4, pred[384,384]{0,1:T(8,128)(4,1)S(1)} %get-tuple-element.234), kind=kLoop, calls=%fused_computation.5 | loop fusion | flops 11790336 | bytes 9633792 | tf_op jit(solution)/shard_map/while/body/eval_jaxpr/cond/branch_1_fun/reduce_sum | solution.py:37
  73.8 0.0 copy-done
  73.8 3.8 %multiply_add_fusion = f32[2,8,384,128]{3,2,1,0:T(8,128)S(1)} fusion(f32[2,8,384,128]{3,2,1,0:T(8,128)S(1)} %copy-done, bf16[384,2,128,1]{0,2,3,1:T(8,128)(2,1)S(1)} %bitcast.37, f32[2,384,384,8]{2,1,3,0:T(8,128)S(1)} %get-tuple-element.332, f32[2,8,384]{2,1,0:T(8,128)S(1)} %max.4, pred[384,384]{0,1:T(8,128)(4,1)S(1)} %get-tuple-element.234, ...), kind=kOutput, calls=%fused_computation.8 | convolution fusion | flops 617349120 | bytes 16121856 | tf_op jit(solution)/shard_map/while/body/eval_jaxpr/cond/branch_1_fun/hgqk,khd->hgqd/dot_general | solution.py:38
  77.6 0.0 copy-start.1
  77.6 1.6 %copy-done.1 = f32[2,8,384,128]{3,2,1,0:T(8,128)} copy-done((f32[2,8,384,128]{3,2,1,0:T(8,128)}, f32[2,8,384,128]{3,2,1,0:T(8,128)S(1)}, u32[]{:S(2)}) %copy-start.1) | copy-done | bytes 3145752 | tf_op jit(solution)/shard_map/while/body/eval_jaxpr/cond
  79.3 0.1 broadcast_compare_fusion.2
  79.4 0.9 fusion.19
  80.9 10.6 %conditional.3 = ((f32[2,8,384]{2,1,0:T(8,128)S(1)}, f32[2,8,384]{2,1,0:T(8,128)S(1)}, f32[2,8,384,128]{3,2,1,0:T(8,128)})) conditional(s32[]{:T(128)} %convert_element_type.33, (f32[2,8,384]{2,1,0:T(8,128)S(1)}, f32[2,8,384]{2,1,0:T(8,128)S(1)}, f32[2,8,384,128]{3,2,1,0:T(8,128)}) %tuple.60, (pred[384,384]{0,1:T(8,128)(4,1)S(1)}, ...), branch_computations={%region_2.0_spmd, %region_3.5_spmd} | conditional | flops 1240215552 | bytes 63357020 | solution.py:46
  80.9 1.1 %constant_dynamic-slice_fusion = (bf16[384,256]{0,1:T(8,128)(2,1)S(1)}, bf16[384,256]{0,1:T(8,128)(2,1)S(1)}) fusion(bf16[1536,256]{0,1:T(8,128)(2,1)} %get-tuple-element.240, s32[]{:T(128)} %get-tuple-element.236, bf16[1536,256]{0,1:T(8,128)(2,1)} %get-tuple-element.235), kind=kLoop, calls=%fused_computation.11 | loop fusion | bytes 786436 | tf_op jit(solution)/shard_map/while/body/eval_jaxpr/dynamic_slice | solution.py:69
  82.0 1.7 %fusion.2 = (f32[2,8,384]{2,1,0:T(8,128)S(1)}, f32[2,384,384,8]{2,1,3,0:T(8,128)S(1)}) fusion(pred[384,384]{0,1:T(8,128)(4,1)S(1)} %get-tuple-element.234, bf16[384,2,128,1]{0,2,3,1:T(8,128)(2,1)S(1)} %bitcast.34, bf16[384,2,8,128]{3,0,2,1:T(8,128)(2,1)S(1)} %get-tuple-element.237), kind=kOutput, calls=%fused_computation.3 | convolution fusion | flops 611051520 | bytes 11378688 | tf_op jit(solution)/shard_map/while/body/eval_jaxpr/cond/branch_1_fun/qhgd,khd->hgqk/dot_general | solution.py:30
  83.7 0.0 copy-start
  83.7 2.3 %fusion.4 = f32[2,8,384]{2,1,0:T(8,128)S(1)} fusion(f32[2,384,384,8]{2,1,3,0:T(8,128)S(1)} %get-tuple-element.332, f32[2,8,384]{2,1,0:T(8,128)S(1)} %max.4, pred[384,384]{0,1:T(8,128)(4,1)S(1)} %get-tuple-element.234), kind=kLoop, calls=%fused_computation.5 | loop fusion | flops 11790336 | bytes 9633792 | tf_op jit(solution)/shard_map/while/body/eval_jaxpr/cond/branch_1_fun/reduce_sum | solution.py:37
  86.0 0.0 copy-done
  86.0 3.8 %multiply_add_fusion = f32[2,8,384,128]{3,2,1,0:T(8,128)S(1)} fusion(f32[2,8,384,128]{3,2,1,0:T(8,128)S(1)} %copy-done, bf16[384,2,128,1]{0,2,3,1:T(8,128)(2,1)S(1)} %bitcast.37, f32[2,384,384,8]{2,1,3,0:T(8,128)S(1)} %get-tuple-element.332, f32[2,8,384]{2,1,0:T(8,128)S(1)} %max.4, pred[384,384]{0,1:T(8,128)(4,1)S(1)} %get-tuple-element.234, ...), kind=kOutput, calls=%fused_computation.8 | convolution fusion | flops 617349120 | bytes 16121856 | tf_op jit(solution)/shard_map/while/body/eval_jaxpr/cond/branch_1_fun/hgqk,khd->hgqd/dot_general | solution.py:38
  89.9 0.0 copy-start.1
  89.9 1.6 %copy-done.1 = f32[2,8,384,128]{3,2,1,0:T(8,128)} copy-done((f32[2,8,384,128]{3,2,1,0:T(8,128)}, f32[2,8,384,128]{3,2,1,0:T(8,128)S(1)}, u32[]{:S(2)}) %copy-start.1) | copy-done | bytes 3145752 | tf_op jit(solution)/shard_map/while/body/eval_jaxpr/cond
  91.5 0.1 broadcast_compare_fusion.2
  91.6 0.9 fusion.19
  93.2 2.4 %fusion.13 = bf16[384,2,8,128]{3,0,2,1:T(8,128)(2,1)S(1)} fusion(f32[2,8,384,128]{3,2,1,0:T(8,128)} %get-tuple-element.257, f32[2,8,384]{2,1,0:T(8,128)S(1)} %get-tuple-element.258), kind=kLoop, calls=%fused_computation.22 | loop fusion | flops 1572864 | bytes 4743168 | tf_op jit(solution)/shard_map/convert_element_type | solution.py:86
  95.6 1.0 %copy.22 = bf16[384,2,8,128]{3,2,1,0:T(8,128)(2,1)S(1)} copy(bf16[384,2,8,128]{3,0,2,1:T(8,128)(2,1)S(1)} %fusion.13) | data formatting | bytes 3145728 | tf_op jit(solution)/shard_map/convert_element_type | solution.py:86
  96.6 1.6 %copy.32 = bf16[48,8,16,128]{3,1,2,0:T(8,128)(2,1)} copy(bf16[48,8,16,128]{3,2,1,0:T(8,128)(2,1)S(1)} %bitcast.35) | data formatting | bytes 3145728
  (18 shorter events, 0.1 us)
Async XLA Ops:
  49.9 4.9 %copy-start.2 = (s32[384]{0:T(512)S(1)}, s32[384]{0:T(512)}, u32[]{:S(2)}) copy-start(s32[384]{0:T(512)} %param.11) | copy-start | bytes 4612
  59.2 2.3 %copy-start = (f32[2,8,384,128]{3,2,1,0:T(8,128)S(1)}, f32[2,8,384,128]{3,2,1,0:T(8,128)}, u32[]{:S(2)}) copy-start(f32[2,8,384,128]{3,2,1,0:T(8,128)} %get-tuple-element.239) | copy-start | bytes 9437188 | tf_op jit(solution)/shard_map/while/body/eval_jaxpr/cond
  65.4 1.7 %copy-start.1 = (f32[2,8,384,128]{3,2,1,0:T(8,128)}, f32[2,8,384,128]{3,2,1,0:T(8,128)S(1)}, u32[]{:S(2)}) copy-start(f32[2,8,384,128]{3,2,1,0:T(8,128)S(1)} %multiply_add_fusion) | copy-start | bytes 9437188 | tf_op jit(solution)/shard_map/while/body/eval_jaxpr/cond
  71.4 2.3 %copy-start = (f32[2,8,384,128]{3,2,1,0:T(8,128)S(1)}, f32[2,8,384,128]{3,2,1,0:T(8,128)}, u32[]{:S(2)}) copy-start(f32[2,8,384,128]{3,2,1,0:T(8,128)} %get-tuple-element.239) | copy-start | bytes 9437188 | tf_op jit(solution)/shard_map/while/body/eval_jaxpr/cond
  77.6 1.7 %copy-start.1 = (f32[2,8,384,128]{3,2,1,0:T(8,128)}, f32[2,8,384,128]{3,2,1,0:T(8,128)S(1)}, u32[]{:S(2)}) copy-start(f32[2,8,384,128]{3,2,1,0:T(8,128)S(1)} %multiply_add_fusion) | copy-start | bytes 9437188 | tf_op jit(solution)/shard_map/while/body/eval_jaxpr/cond
  83.7 2.3 %copy-start = (f32[2,8,384,128]{3,2,1,0:T(8,128)S(1)}, f32[2,8,384,128]{3,2,1,0:T(8,128)}, u32[]{:S(2)}) copy-start(f32[2,8,384,128]{3,2,1,0:T(8,128)} %get-tuple-element.239) | copy-start | bytes 9437188 | tf_op jit(solution)/shard_map/while/body/eval_jaxpr/cond
  89.9 1.7 %copy-start.1 = (f32[2,8,384,128]{3,2,1,0:T(8,128)}, f32[2,8,384,128]{3,2,1,0:T(8,128)S(1)}, u32[]{:S(2)}) copy-start(f32[2,8,384,128]{3,2,1,0:T(8,128)S(1)} %multiply_add_fusion) | copy-start | bytes 9437188 | tf_op jit(solution)/shard_map/while/body/eval_jaxpr/cond
where the time goes:
time: 98.4 us; the launch traced here: 98.1 us
  blocking collectives  47 us (48%)
  local copies, waits for them, and re-layouts  18.5 us (19%)
  matrix products  16.6 us (17%)
  other arithmetic  13.2 us (13%)
  loops' own time  2.79 us (3%)
    all_gather x1, blocking collectives, per_device(): value_all = lax.all_gather(values, 'ctx', axis=0, tiled=True)  18.8 us
    all_gather x1, blocking collectives, per_device(): key_all = lax.all_gather(keys, 'ctx', axis=0, tiled=True)  17.9 us
    dot_general x3, matrix products, compute(): jnp.einsum('hgqk,khd->hgqd', weights.astype(jnp.bfloat16), value_heads, p...  11.5 us
    all_gather x1, blocking collectives, per_device(): segment_all = lax.all_gather(segment_ids, 'ctx', axis=0, tiled=True)  10.3 us
    unnamed x9, local copies, waits for them, and re-layouts  7.27 us
    reduce_sum x3, other arithmetic, compute(): new_total = row_total * factor + jnp.sum(weights, axis=-1)  6.83 us
    dot_general x3, matrix products, compute(): jnp.einsum('qhgd,khd->hgqk', query_heads, key_heads, preferred_element_ty...  5.11 us
    cond x15, local copies, waits for them, and re-layouts  4.98 us

commit v1 on v0

--- a/solution.py
+++ b/solution.py
@@ -1,3 +1,4 @@
+import functools
 import jax
 import jax.numpy as jnp
 from jax import lax
@@ -5,6 +6,23 @@
 
 HEAD_DIM = 128
 GROUP = 8
+
+
+def post_loops(array_here, along_dim):
+    count_all = lax.axis_size("ctx")
+    lower = range(count_all)
+    found_now = map(lambda i: (i, (i + 1) % count_all), lower)
+    last = [None] * count_all
+    last[count_all - 1] = array_here
+    bank = list(found_now)
+    for k in range(count_all - 2, -1, -1):
+        last[k] = lax.ppermute(last[k + 1], "ctx", perm=bank)
+    block_next = jnp.concatenate(last, along_dim)
+    outer = lax.axis_index("ctx")
+    return jnp.roll(block_next, (outer + 1) * array_here.shape[along_dim], along_dim)
+
+
+refer_goods = functools.partial(post_loops, along_dim=0)
 
 
 def attend_block(
@@ -57,7 +75,7 @@
         jnp.zeros((heads_here, GROUP, row_count), jnp.float32),
         jnp.zeros((heads_here, GROUP, row_count, HEAD_DIM), jnp.float32),
     )
-    key_all = lax.all_gather(keys, "ctx", axis=0, tiled=True)
+    key_all = refer_goods(keys)
     value_all = lax.all_gather(values, "ctx", axis=0, tiled=True)
     segment_all = lax.all_gather(segment_ids, "ctx", axis=0, tiled=True)
     blocks = max(1, key_all.shape[0] // row_count)

time: 98.4 us -> 91.4 us (0.929)
  blocking collectives: 47 us -> 30.4 us
  waiting for transfers between devices: 0 us -> 5.07 us
  starting transfers between devices: 0 us -> 4.46 us
    all_gather x1 -> x0, blocking collectives: 17.9 us -> none  [per_device(): key_all = lax.all_gather(keys, 'ctx', axis=0, tiled=True)]
    ppermute x0 -> x3, waiting for transfers between devices: none -> 5.07 us  [post_loops(): last[k] = lax.ppermute(last[k + 1], 'ctx', perm=bank)]
    ppermute x0 -> x3, starting transfers between devices: none -> 4.46 us  [post_loops(): last[k] = lax.ppermute(last[k + 1], 'ctx', perm=bank)]
    dynamic_slice x3, local copies, waits for them, and re-layouts: 3.21 us -> 0.15 us  [turn(): value_part = lax.dynamic_slice_in_dim(value_all, offset, width_rows, 0)]
    unnamed x9 -> x16, local copies, waits for them, and re-layouts: 7.27 us -> 10 us
    all_gather x1, blocking collectives: 10.3 us -> 11.5 us  [per_device(): segment_all = lax.all_gather(segment_ids, 'ctx', axis=0, tiled=True)]
  transfers between devices with their start and end apart: 0 -> 3, of which waited for: 0 -> 1; matrix products, arithmetic and copies ran while one was open for 0% -> 6% of each run, Pallas kernels for 0% -> 0%
where the time goes in v1:
time: 91.4 us; the launch traced here: 90.7 us
  blocking collectives  30.4 us (33%)
  local copies, waits for them, and re-layouts  18.5 us (20%)
  matrix products  16.4 us (18%)
  other arithmetic  13.2 us (14%)
  waiting for transfers between devices  5.07 us (6%)
  starting transfers between devices  4.46 us (5%)
  loops' own time  2.55 us (3%)
    all_gather x1, blocking collectives, per_device(): value_all = lax.all_gather(values, 'ctx', axis=0, tiled=True)  18.9 us
    all_gather x1, blocking collectives, per_device(): segment_all = lax.all_gather(segment_ids, 'ctx', axis=0, tiled=True)  11.5 us
    dot_general x3, matrix products, compute(): jnp.einsum('hgqk,khd->hgqd', weights.astype(jnp.bfloat16), value_heads, p...  11.3 us
    unnamed x16, local copies, waits for them, and re-layouts  10 us
    reduce_sum x3, other arithmetic, compute(): new_total = row_total * factor + jnp.sum(weights, axis=-1)  6.83 us
    dot_general x3, matrix products, compute(): jnp.einsum('qhgd,khd->hgqk', query_heads, key_heads, preferred_element_ty...  5.11 us
    ppermute x3, waiting for transfers between devices, post_loops(): last[k] = lax.ppermute(last[k + 1], 'ctx', perm=bank)  5.07 us
    cond x15, local copies, waits for them, and re-layouts  4.93 us
  transfers between devices with their start and end apart: 3, of which 1 were waited for; matrix products, arithmetic and copies ran while one was open for 6% of the time, Pallas kernels for 0%

profile of v1, /device:TPU:22, one launch (start us, length us, event | category | flops | bytes accessed | tf_op | source)
XLA Modules:
  0.0 90.7 jit_solution(17125387557320996801)
XLA Ops:
  0.0 1.1 %copy.20 = bf16[384,256]{0,1:T(8,128)(2,1)S(1)} copy(bf16[384,256]{1,0:T(8,128)(2,1)} %param.9) | data formatting | bytes 393216 | tf_op args[1]
  1.1 1.6 %collective-permute-start = (bf16[384,256]{0,1:T(8,128)(2,1)S(1)}, bf16[384,256]{0,1:T(8,128)(2,1)S(1)}, u32[]{:S(2)}, u32[]{:S(2)}) collective-permute-start(bf16[384,256]{0,1:T(8,128)(2,1)S(1)} %copy.20), channel_id=1, source_target_pairs={{0,4},{4,8},{8,12},{12,0},{1,5},{5,9},{9,13},{13,1},{2,6},{6,10},{... | collective-permute-start | bytes 589832 | tf_op jit(solution)/shard_map/ppermute | solution.py:19
  2.7 5.1 %collective-permute-done = bf16[384,256]{0,1:T(8,128)(2,1)S(1)} collective-permute-done((bf16[384,256]{0,1:T(8,128)(2,1)S(1)}, bf16[384,256]{0,1:T(8,128)(2,1)S(1)}, u32[]{:S(2)}, u32[]{:S(2)}) %collective-permute-start) | collective-permute-done | bytes 196640 | tf_op jit(solution)/shard_map/ppermute | solution.py:19
  7.8 1.6 %collective-permute-start.1 = (bf16[384,256]{0,1:T(8,128)(2,1)S(1)}, bf16[384,256]{0,1:T(8,128)(2,1)}, u32[]{:S(2)}, u32[]{:S(2)}) collective-permute-start(bf16[384,256]{0,1:T(8,128)(2,1)S(1)} %collective-permute-done), channel_id=1, source_target_pairs={{0,4},{4,8},{8,12},{12,0},{1,5},{5,9},{9,13},{13,1},{2,6},{6,10},{... | collective-permute-start | bytes 589832 | tf_op jit(solution)/shard_map/ppermute | solution.py:19
  9.4 0.7 reshape.39
  10.0 11.5 %all-gather = s32[4,1,384]{2,1,0:T(1,128)S(1)} all-gather(s32[1,1,384]{2,1,0:T(1,128)S(1)} %reshape.39), channel_id=1, replica_groups=mesh['groups'=2,'ctx'=4,'tp'=2,'sub'=2] {'ctx'}, dimensions={0}, use_global_device_ids=true | all-gather | bytes 7680 | tf_op jit(solution)/shard_map/all_gather | solution.py:80
  21.6 1.7 %copy.24 = bf16[384,256]{0,1:T(8,128)(2,1)} copy(bf16[384,256]{1,0:T(8,128)(2,1)} %param.10) | data formatting | bytes 393216 | tf_op args[2]
  23.3 1.9 %copy.23 = bf16[384,2048]{0,1:T(8,128)(2,1)S(1)} copy(bf16[384,2048]{1,0:T(8,128)(2,1)} %param.8) | data formatting | bytes 3145728 | tf_op args[0]
  25.2 1.0 %copy.25 = bf16[384,2,8,128]{3,0,2,1:T(8,128)(2,1)S(1)} copy(bf16[384,2,8,128]{0,3,2,1:T(8,128)(2,1)S(1)} %bitcast.36) | data formatting | bytes 3145728
  26.2 0.0 collective-permute-done.1
  26.2 1.3 %collective-permute-start.2 = (bf16[384,256]{0,1:T(8,128)(2,1)}, bf16[384,256]{0,1:T(8,128)(2,1)S(1)}, u32[]{:S(2)}, u32[]{:S(2)}) collective-permute-start(bf16[384,256]{0,1:T(8,128)(2,1)} %collective-permute-done.1), channel_id=1, source_target_pairs={{0,4},{4,8},{8,12},{12,0},{1,5},{5,9},{9,13},{13,1},{2,6},{6,10},{... | collective-permute-start | bytes 589832 | tf_op jit(solution)/shard_map/ppermute | solution.py:19
  27.4 18.9 %all_gather.7 = bf16[1536,256]{0,1:T(8,128)(2,1)S(1)} all-gather(bf16[384,256]{0,1:T(8,128)(2,1)} %copy.24), channel_id=1, replica_groups=mesh['groups'=2,'ctx'=4,'tp'=2,'sub'=2] {'ctx'}, dimensions={0}, use_global_device_ids=true | all-gather | bytes 983040 | tf_op jit(solution)/shard_map/all_gather | solution.py:79
  46.4 0.0 collective-permute-done.2
  46.4 1.0 %constant_dynamic-update-slice_fusion.6 = bf16[3072,256]{0,1:T(8,128)(2,1)S(1)} fusion(bf16[3072,256]{0,1:T(8,128)(2,1)S(1)} %constant_dynamic-update-slice_fusion.7, bf16[384,256]{0,1:T(8,128)(2,1)} %collective-permute-done.1), kind=kLoop, calls=%fused_computation.29 | loop fusion | bytes 393216
  47.5 0.0 copy-start.2
  47.5 1.0 %constant_dynamic-update-slice_fusion.2 = bf16[3072,256]{0,1:T(8,128)(2,1)S(1)} fusion(bf16[3072,256]{0,1:T(8,128)(2,1)S(1)} %constant_dynamic-update-slice_fusion.3, bf16[384,256]{0,1:T(8,128)(2,1)} %collective-permute-done.1), kind=kLoop, calls=%fused_computation.25 | loop fusion | bytes 393216
  48.6 0.3 constant_dynamic-slice_fusion.2
  49.0 2.0 %broadcast_in_dim.53 = f32[2,8,384,128]{3,2,1,0:T(8,128)} broadcast(f32[]{:T(128)} %constant.85.clone.1), dimensions={} | broadcast | bytes 3145732 | tf_op jit(solution)/shard_map/broadcast_in_dim | solution.py:76
  50.9 0.0 copy-done.2
  50.9 34.8 %while.18 = (s32[]{:T(128)}, f32[2,8,384]{2,1,0:T(8,128)S(1)}, f32[2,8,384]{2,1,0:T(8,128)S(1)}, f32[2,8,384,128]{3,2,1,0:T(8,128)}, s32[1536]{0:T(1024)S(1)}, /...) while((s32[]{:T(128)}, f32[2,8,384]{2,1,0:T(8,128)S(1)}, ...), condition=%wide.region_6.7_spmd.clone, body=%wide.region_0.6_spmd.clone.sunk | while | flops 1240953984 | bytes 63517816 | solution.py:100
  50.9 0.1 broadcast_compare_fusion.2
  51.0 0.9 fusion.19
  52.5 9.5 %conditional.3 = ((f32[2,8,384]{2,1,0:T(8,128)S(1)}, f32[2,8,384]{2,1,0:T(8,128)S(1)}, f32[2,8,384,128]{3,2,1,0:T(8,128)})) conditional(s32[]{:T(128)} %convert_element_type.33, (f32[2,8,384]{2,1,0:T(8,128)S(1)}, f32[2,8,384]{2,1,0:T(8,128)S(1)}, f32[2,8,384,128]{3,2,1,0:T(8,128)}) %tuple.60, (pred[384,384]{0,1:T(8,128)(4,1)S(1)}, ...), branch_computations={%region_2.2_spmd, %region_3.5_spmd} | conditional | flops 1240215552 | bytes 63357020 | solution.py:64
  52.5 0.1 constant_dynamic-slice_fusion
  52.5 1.7 %fusion.2 = (f32[2,8,384]{2,1,0:T(8,128)S(1)}, f32[2,384,384,8]{2,1,3,0:T(8,128)S(1)}) fusion(pred[384,384]{0,1:T(8,128)(4,1)S(1)} %get-tuple-element.234, bf16[384,2,128,1]{0,2,3,1:T(8,128)(2,1)S(1)} %bitcast.34, bf16[384,2,8,128]{3,0,2,1:T(8,128)(2,1)S(1)} %get-tuple-element.237), kind=kOutput, calls=%fused_computation.3 | convolution fusion | flops 611051520 | bytes 11378688 | tf_op jit(solution)/shard_map/while/body/eval_jaxpr/cond/branch_1_fun/qhgd,khd->hgqk/dot_general | solution.py:48
  54.3 0.0 copy-start
  54.3 2.3 %fusion.4 = f32[2,8,384]{2,1,0:T(8,128)S(1)} fusion(f32[2,384,384,8]{2,1,3,0:T(8,128)S(1)} %get-tuple-element.332, f32[2,8,384]{2,1,0:T(8,128)S(1)} %max.4, pred[384,384]{0,1:T(8,128)(4,1)S(1)} %get-tuple-element.234), kind=kLoop, calls=%fused_computation.5 | loop fusion | flops 11790336 | bytes 9633792 | tf_op jit(solution)/shard_map/while/body/eval_jaxpr/cond/branch_1_fun/reduce_sum | solution.py:55
  56.6 0.0 copy-done
  56.6 3.8 %multiply_add_fusion = f32[2,8,384,128]{3,2,1,0:T(8,128)S(1)} fusion(f32[2,8,384,128]{3,2,1,0:T(8,128)S(1)} %copy-done, bf16[384,2,128,1]{0,2,3,1:T(8,128)(2,1)S(1)} %bitcast.37, f32[2,384,384,8]{2,1,3,0:T(8,128)S(1)} %get-tuple-element.332, f32[2,8,384]{2,1,0:T(8,128)S(1)} %max.4, pred[384,384]{0,1:T(8,128)(4,1)S(1)} %get-tuple-element.234, ...), kind=kOutput, calls=%fused_computation.8 | convolution fusion | flops 617349120 | bytes 16121856 | tf_op jit(solution)/shard_map/while/body/eval_jaxpr/cond/branch_1_fun/hgqk,khd->hgqd/dot_general | solution.py:56
  60.4 0.0 copy-start.1
  60.4 1.6 %copy-done.1 = f32[2,8,384,128]{3,2,1,0:T(8,128)} copy-done((f32[2,8,384,128]{3,2,1,0:T(8,128)}, f32[2,8,384,128]{3,2,1,0:T(8,128)S(1)}, u32[]{:S(2)}) %copy-start.1) | copy-done | bytes 3145752 | tf_op jit(solution)/shard_map/while/body/eval_jaxpr/cond
  62.0 0.1 broadcast_compare_fusion.2
  62.1 0.9 fusion.19
  63.5 9.5 %conditional.3 = ((f32[2,8,384]{2,1,0:T(8,128)S(1)}, f32[2,8,384]{2,1,0:T(8,128)S(1)}, f32[2,8,384,128]{3,2,1,0:T(8,128)})) conditional(s32[]{:T(128)} %convert_element_type.33, (f32[2,8,384]{2,1,0:T(8,128)S(1)}, f32[2,8,384]{2,1,0:T(8,128)S(1)}, f32[2,8,384,128]{3,2,1,0:T(8,128)}) %tuple.60, (pred[384,384]{0,1:T(8,128)(4,1)S(1)}, ...), branch_computations={%region_2.2_spmd, %region_3.5_spmd} | conditional | flops 1240215552 | bytes 63357020 | solution.py:64
  63.6 0.1 constant_dynamic-slice_fusion
  63.6 1.7 %fusion.2 = (f32[2,8,384]{2,1,0:T(8,128)S(1)}, f32[2,384,384,8]{2,1,3,0:T(8,128)S(1)}) fusion(pred[384,384]{0,1:T(8,128)(4,1)S(1)} %get-tuple-element.234, bf16[384,2,128,1]{0,2,3,1:T(8,128)(2,1)S(1)} %bitcast.34, bf16[384,2,8,128]{3,0,2,1:T(8,128)(2,1)S(1)} %get-tuple-element.237), kind=kOutput, calls=%fused_computation.3 | convolution fusion | flops 611051520 | bytes 11378688 | tf_op jit(solution)/shard_map/while/body/eval_jaxpr/cond/branch_1_fun/qhgd,khd->hgqk/dot_general | solution.py:48
  65.3 0.0 copy-start
  65.3 2.3 %fusion.4 = f32[2,8,384]{2,1,0:T(8,128)S(1)} fusion(f32[2,384,384,8]{2,1,3,0:T(8,128)S(1)} %get-tuple-element.332, f32[2,8,384]{2,1,0:T(8,128)S(1)} %max.4, pred[384,384]{0,1:T(8,128)(4,1)S(1)} %get-tuple-element.234), kind=kLoop, calls=%fused_computation.5 | loop fusion | flops 11790336 | bytes 9633792 | tf_op jit(solution)/shard_map/while/body/eval_jaxpr/cond/branch_1_fun/reduce_sum | solution.py:55
  67.7 0.0 copy-done
  67.7 3.8 %multiply_add_fusion = f32[2,8,384,128]{3,2,1,0:T(8,128)S(1)} fusion(f32[2,8,384,128]{3,2,1,0:T(8,128)S(1)} %copy-done, bf16[384,2,128,1]{0,2,3,1:T(8,128)(2,1)S(1)} %bitcast.37, f32[2,384,384,8]{2,1,3,0:T(8,128)S(1)} %get-tuple-element.332, f32[2,8,384]{2,1,0:T(8,128)S(1)} %max.4, pred[384,384]{0,1:T(8,128)(4,1)S(1)} %get-tuple-element.234, ...), kind=kOutput, calls=%fused_computation.8 | convolution fusion | flops 617349120 | bytes 16121856 | tf_op jit(solution)/shard_map/while/body/eval_jaxpr/cond/branch_1_fun/hgqk,khd->hgqd/dot_general | solution.py:56
  71.4 0.0 copy-start.1
  71.4 1.6 %copy-done.1 = f32[2,8,384,128]{3,2,1,0:T(8,128)} copy-done((f32[2,8,384,128]{3,2,1,0:T(8,128)}, f32[2,8,384,128]{3,2,1,0:T(8,128)S(1)}, u32[]{:S(2)}) %copy-start.1) | copy-done | bytes 3145752 | tf_op jit(solution)/shard_map/while/body/eval_jaxpr/cond
  73.1 0.1 broadcast_compare_fusion.2
  73.2 0.9 fusion.19
  74.6 9.5 %conditional.3 = ((f32[2,8,384]{2,1,0:T(8,128)S(1)}, f32[2,8,384]{2,1,0:T(8,128)S(1)}, f32[2,8,384,128]{3,2,1,0:T(8,128)})) conditional(s32[]{:T(128)} %convert_element_type.33, (f32[2,8,384]{2,1,0:T(8,128)S(1)}, f32[2,8,384]{2,1,0:T(8,128)S(1)}, f32[2,8,384,128]{3,2,1,0:T(8,128)}) %tuple.60, (pred[384,384]{0,1:T(8,128)(4,1)S(1)}, ...), branch_computations={%region_2.2_spmd, %region_3.5_spmd} | conditional | flops 1240215552 | bytes 63357020 | solution.py:64
  74.6 0.1 constant_dynamic-slice_fusion
  74.7 1.7 %fusion.2 = (f32[2,8,384]{2,1,0:T(8,128)S(1)}, f32[2,384,384,8]{2,1,3,0:T(8,128)S(1)}) fusion(pred[384,384]{0,1:T(8,128)(4,1)S(1)} %get-tuple-element.234, bf16[384,2,128,1]{0,2,3,1:T(8,128)(2,1)S(1)} %bitcast.34, bf16[384,2,8,128]{3,0,2,1:T(8,128)(2,1)S(1)} %get-tuple-element.237), kind=kOutput, calls=%fused_computation.3 | convolution fusion | flops 611051520 | bytes 11378688 | tf_op jit(solution)/shard_map/while/body/eval_jaxpr/cond/branch_1_fun/qhgd,khd->hgqk/dot_general | solution.py:48
  76.4 0.0 copy-start
  76.4 2.3 %fusion.4 = f32[2,8,384]{2,1,0:T(8,128)S(1)} fusion(f32[2,384,384,8]{2,1,3,0:T(8,128)S(1)} %get-tuple-element.332, f32[2,8,384]{2,1,0:T(8,128)S(1)} %max.4, pred[384,384]{0,1:T(8,128)(4,1)S(1)} %get-tuple-element.234), kind=kLoop, calls=%fused_computation.5 | loop fusion | flops 11790336 | bytes 9633792 | tf_op jit(solution)/shard_map/while/body/eval_jaxpr/cond/branch_1_fun/reduce_sum | solution.py:55
  78.7 0.0 copy-done
  78.7 3.8 %multiply_add_fusion = f32[2,8,384,128]{3,2,1,0:T(8,128)S(1)} fusion(f32[2,8,384,128]{3,2,1,0:T(8,128)S(1)} %copy-done, bf16[384,2,128,1]{0,2,3,1:T(8,128)(2,1)S(1)} %bitcast.37, f32[2,384,384,8]{2,1,3,0:T(8,128)S(1)} %get-tuple-element.332, f32[2,8,384]{2,1,0:T(8,128)S(1)} %max.4, pred[384,384]{0,1:T(8,128)(4,1)S(1)} %get-tuple-element.234, ...), kind=kOutput, calls=%fused_computation.8 | convolution fusion | flops 617349120 | bytes 16121856 | tf_op jit(solution)/shard_map/while/body/eval_jaxpr/cond/branch_1_fun/hgqk,khd->hgqd/dot_general | solution.py:56
  82.5 0.0 copy-start.1
  82.5 1.6 %copy-done.1 = f32[2,8,384,128]{3,2,1,0:T(8,128)} copy-done((f32[2,8,384,128]{3,2,1,0:T(8,128)}, f32[2,8,384,128]{3,2,1,0:T(8,128)S(1)}, u32[]{:S(2)}) %copy-start.1) | copy-done | bytes 3145752 | tf_op jit(solution)/shard_map/while/body/eval_jaxpr/cond
  84.1 0.1 broadcast_compare_fusion.2
  84.2 0.9 fusion.19
  85.7 2.4 %fusion.13 = bf16[384,2,8,128]{3,0,2,1:T(8,128)(2,1)S(1)} fusion(f32[2,8,384,128]{3,2,1,0:T(8,128)} %get-tuple-element.257, f32[2,8,384]{2,1,0:T(8,128)S(1)} %get-tuple-element.258), kind=kLoop, calls=%fused_computation.22 | loop fusion | flops 1572864 | bytes 4743168 | tf_op jit(solution)/shard_map/convert_element_type | solution.py:104
  88.1 1.0 %copy.26 = bf16[384,2,8,128]{3,2,1,0:T(8,128)(2,1)S(1)} copy(bf16[384,2,8,128]{3,0,2,1:T(8,128)(2,1)S(1)} %fusion.13) | data formatting | bytes 3145728 | tf_op jit(solution)/shard_map/convert_element_type | solution.py:104
  89.1 1.6 %copy.36 = bf16[48,8,16,128]{3,1,2,0:T(8,128)(2,1)} copy(bf16[48,8,16,128]{3,2,1,0:T(8,128)(2,1)S(1)} %bitcast.35) | data formatting | bytes 3145728
  (24 shorter events, 0.4 us)
Async XLA Ops:
  1.1 6.7 %collective-permute-start = (bf16[384,256]{0,1:T(8,128)(2,1)S(1)}, bf16[384,256]{0,1:T(8,128)(2,1)S(1)}, u32[]{:S(2)}, u32[]{:S(2)}) collective-permute-start(bf16[384,256]{0,1:T(8,128)(2,1)S(1)} %copy.20), channel_id=1, source_target_pairs={{0,4},{4,8},{8,12},{12,0},{1,5},{5,9},{9,13},{13,1},{2,6},{6,10},{... | collective-permute-start | bytes 589832 | tf_op jit(solution)/shard_map/ppermute | solution.py:19
  7.8 18.4 %collective-permute-start.1 = (bf16[384,256]{0,1:T(8,128)(2,1)S(1)}, bf16[384,256]{0,1:T(8,128)(2,1)}, u32[]{:S(2)}, u32[]{:S(2)}) collective-permute-start(bf16[384,256]{0,1:T(8,128)(2,1)S(1)} %collective-permute-done), channel_id=1, source_target_pairs={{0,4},{4,8},{8,12},{12,0},{1,5},{5,9},{9,13},{13,1},{2,6},{6,10},{... | collective-permute-start | bytes 589832 | tf_op jit(solution)/shard_map/ppermute | solution.py:19
  26.2 20.2 %collective-permute-start.2 = (bf16[384,256]{0,1:T(8,128)(2,1)}, bf16[384,256]{0,1:T(8,128)(2,1)S(1)}, u32[]{:S(2)}, u32[]{:S(2)}) collective-permute-start(bf16[384,256]{0,1:T(8,128)(2,1)} %collective-permute-done.1), channel_id=1, source_target_pairs={{0,4},{4,8},{8,12},{12,0},{1,5},{5,9},{9,13},{13,1},{2,6},{6,10},{... | collective-permute-start | bytes 589832 | tf_op jit(solution)/shard_map/ppermute | solution.py:19
  47.5 3.5 %copy-start.2 = (s32[384]{0:T(512)S(1)}, s32[384]{0:T(512)}, u32[]{:S(2)}) copy-start(s32[384]{0:T(512)} %param.11) | copy-start | bytes 4612
  54.3 2.3 %copy-start = (f32[2,8,384,128]{3,2,1,0:T(8,128)S(1)}, f32[2,8,384,128]{3,2,1,0:T(8,128)}, u32[]{:S(2)}) copy-start(f32[2,8,384,128]{3,2,1,0:T(8,128)} %get-tuple-element.239) | copy-start | bytes 9437188 | tf_op jit(solution)/shard_map/while/body/eval_jaxpr/cond
  60.4 1.6 %copy-start.1 = (f32[2,8,384,128]{3,2,1,0:T(8,128)}, f32[2,8,384,128]{3,2,1,0:T(8,128)S(1)}, u32[]{:S(2)}) copy-start(f32[2,8,384,128]{3,2,1,0:T(8,128)S(1)} %multiply_add_fusion) | copy-start | bytes 9437188 | tf_op jit(solution)/shard_map/while/body/eval_jaxpr/cond
  65.3 2.3 %copy-start = (f32[2,8,384,128]{3,2,1,0:T(8,128)S(1)}, f32[2,8,384,128]{3,2,1,0:T(8,128)}, u32[]{:S(2)}) copy-start(f32[2,8,384,128]{3,2,1,0:T(8,128)} %get-tuple-element.239) | copy-start | bytes 9437188 | tf_op jit(solution)/shard_map/while/body/eval_jaxpr/cond
  71.4 1.6 %copy-start.1 = (f32[2,8,384,128]{3,2,1,0:T(8,128)}, f32[2,8,384,128]{3,2,1,0:T(8,128)S(1)}, u32[]{:S(2)}) copy-start(f32[2,8,384,128]{3,2,1,0:T(8,128)S(1)} %multiply_add_fusion) | copy-start | bytes 9437188 | tf_op jit(solution)/shard_map/while/body/eval_jaxpr/cond
  76.4 2.3 %copy-start = (f32[2,8,384,128]{3,2,1,0:T(8,128)S(1)}, f32[2,8,384,128]{3,2,1,0:T(8,128)}, u32[]{:S(2)}) copy-start(f32[2,8,384,128]{3,2,1,0:T(8,128)} %get-tuple-element.239) | copy-start | bytes 9437188 | tf_op jit(solution)/shard_map/while/body/eval_jaxpr/cond
  82.5 1.6 %copy-start.1 = (f32[2,8,384,128]{3,2,1,0:T(8,128)}, f32[2,8,384,128]{3,2,1,0:T(8,128)S(1)}, u32[]{:S(2)}) copy-start(f32[2,8,384,128]{3,2,1,0:T(8,128)S(1)} %multiply_add_fusion) | copy-start | bytes 9437188 | tf_op jit(solution)/shard_map/while/body/eval_jaxpr/cond
